TPU v7x, 32 devices: a whole 2x2x4 slice. The times are simulated.
32 devices in a mesh: ma: 16 (over z, y, x), ch: 2 (over core).
Axes of the slice: x: 2, y: 2, z: 4, core: 2. Of those that a mesh axis runs over, the one named last changes fastest.
Arguments:
- visibilities: bfloat16 [512, 512, 2, 128], P('ma', 'ch'), may hold values from -6 to 6
- kl_basis: bfloat16 [512, 256, 2, 512], P('ma', 'ch'), may hold values from -0.1875 to 0.1875
- time_flags: int32 [512], P('ma'), may hold values 0 or 1
Outputs:
- kl_modes: bfloat16 [512, 256, 2, 128], P('ma', 'ch')
All inputs are finite; a program needn't handle non-finite values. No bound on the sum of `time_flags` on one device may be relied on, other than what follows from the above.
Results may differ from a plain program's by a relative error of at most 0.006.
Values may be sent and summed in bfloat16 or wider, within the bound.
No kernel may reach another device: no remote copies, remote signals or barrier semaphores. Data moves between devices by JAX's collectives and lax.ppermute only.
A program may use at most 128 MiB of HBM per device.

v0:
```python
import math
import jax
import jax.numpy as jnp
from jax import lax
from jax.sharding import PartitionSpec as P

H = 128


def tap_table(offsets, total):
    shifts = jnp.mod(jnp.arange(2 * H + 1, dtype=jnp.int32) - H, total)
    phase_index = jnp.mod(shifts[:, None] * offsets[None, :], total)
    phases = phase_index.astype(jnp.float32) * (2.0 * math.pi / total)
    return (jnp.cos(phases), jnp.sin(phases))


def toeplitz(kernel_taps, block_rows):
    width = kernel_taps.shape[1]
    span = block_rows + width - 1
    reverse = kernel_taps[:, ::-1]
    padded = jnp.concatenate([reverse, jnp.zeros((2, block_rows), kernel_taps.dtype)], axis=1)
    tiled = jnp.tile(padded, (1, block_rows))[:, : block_rows * span].reshape(2, block_rows, span)
    real_part = tiled[0]
    imag_part = tiled[1]
    first = jnp.stack([real_part, -imag_part], 1)
    second = jnp.stack([imag_part, real_part], 1)
    return jnp.stack([first, second], 0)


def on_device(visibilities, kl_basis, time_flags):
    rows_dev = visibilities.shape[0]
    chan_dev = visibilities.shape[1]
    svd_modes = visibilities.shape[3]
    total = rows_dev * lax.axis_size("ma")
    all_flags = lax.all_gather(time_flags, "ma", axis=0, tiled=True)
    cosine, sine_table = tap_table(jnp.arange(total, dtype=jnp.int32), total)
    flag_values = all_flags.astype(jnp.float32)
    real_sum = jnp.dot(cosine, flag_values, precision=lax.Precision.HIGHEST)
    imag_sum = jnp.dot(sine_table, flag_values, precision=lax.Precision.HIGHEST)
    kernel_taps = (jnp.stack([real_sum, -imag_sum]) / total).astype(jnp.bfloat16)
    flat_rows = jnp.transpose(visibilities, (0, 2, 1, 3)).reshape(rows_dev, 2, chan_dev * svd_modes)
    columns = lax.all_to_all(flat_rows, "ma", split_axis=2, concat_axis=0, tiled=True)
    block_rows = math.gcd(total, 128)
    toeplitz_block = toeplitz(kernel_taps, block_rows)
    wrapped = jnp.concatenate([columns[total - H :], columns, columns[:H]], axis=0)

    def convolve(block_index):
        window = lax.dynamic_slice_in_dim(wrapped, block_index * block_rows, block_rows + 2 * H, 0)
        return jnp.einsum(
            "pbqe,eqf->bpf", toeplitz_block, window, preferred_element_type=jnp.float32
        ).astype(jnp.bfloat16)

    mixed_blocks = lax.map(convolve, jnp.arange(total // block_rows, dtype=jnp.int32))
    mixed_columns = mixed_blocks.reshape(total, 2, columns.shape[2])
    returned = lax.all_to_all(mixed_columns, "ma", split_axis=0, concat_axis=2, tiled=True)
    mixed_rows = jnp.transpose(returned.reshape(rows_dev, 2, chan_dev, svd_modes), (0, 2, 1, 3))
    products = jnp.einsum(
        "mkqc,mcrs->mkqrs",
        kl_basis,
        lax.all_gather(mixed_rows, "ch", axis=1, tiled=True),
        preferred_element_type=jnp.float32,
    )
    real_out = products[:, :, 0, 0, :] - products[:, :, 1, 1, :]
    imag_out = products[:, :, 0, 1, :] + products[:, :, 1, 0, :]
    return jnp.stack([real_out, imag_out], 2).astype(jnp.bfloat16)


def solution(mesh):
    return jax.shard_map(
        on_device,
        mesh=mesh,
        in_specs=(P("ma", "ch", None, None), P("ma", "ch", None, None), P("ma")),
        out_specs=P("ma", "ch", None, None),
        check_vma=False,
    )
```

profile of v0, /device:TPU:0, one launch (start us, length us, event | category | flops | bytes accessed | tf_op | source)
XLA Modules:
  0.0 460.7 jit_solution(17408753481748408428)
XLA Ops:
  6.5 40.5 %copy.49 = bf16[32,2,256,128]{0,1,3,2:T(2,128)(2,1)} copy(bf16[32,2,256,128]{3,1,2,0:T(2,128)(2,1)} %bitcast.99) | data formatting | bytes 8388608 | tf_op jit(solution)/shard_map/reshape | solution.py:41
  47.0 20.8 %reshape.107 = bf16[16,2,65536]{2,1,0:T(2,128)(2,1)} reshape(bf16[32768,2,32]{2,1,0:T(2,128)(2,1)} %bitcast.92) | data formatting | bytes 8388608
  67.8 8.5 %all-to-all-start = ((bf16[16,2,65536]{2,1,0:T(2,128)(2,1)}), bf16[16,2,65536]{2,1,0:T(2,128)(2,1)}, u32[]{:S(2)}, u32[]{:S(2)}) async-start(bf16[16,2,65536]{2,1,0:T(2,128)(2,1)} %reshape.107), calls=%async_computation | async-start | bytes 8388608 | tf_op jit(solution)/shard_map/all_to_all | solution.py:42
  77.8 91.8 %all-reduce.1 = s32[512]{0:T(512)S(1)} all-reduce(s32[512]{0:T(512)S(1)} %dynamic-update-slice), channel_id=1, replica_groups=mesh['ma'=16,'ch'=2] {'ma'}, use_global_device_ids=true, to_apply=%add.1 | all-reduce | flops 512 | bytes 4096
  169.6 2.6 convolution_reduce_fusion
  172.2 2.5 fusion.30
  175.4 0.7 tile.10
  176.1 1.0 slice_reduce_fusion
  177.4 16.0 %reshape.108 = bf16[32768,2,32]{2,1,0:T(2,128)(2,1)} reshape(bf16[16,2,65536]{2,1,0:T(2,128)(2,1)} %all-to-all-done) | data formatting | bytes 8388608
  193.4 24.9 %copy.50 = bf16[32,2,16,2048]{3,2,0,1:T(8,128)(2,1)} copy(bf16[32,2,16,2048]{0,1,3,2:T(2,128)(2,1)} %bitcast.90) | data formatting | bytes 8388608 | tf_op jit(solution)/shard_map/all_to_all | solution.py:42
  218.3 38.2 %copy.51 = bf16[32,2,16,2048]{3,0,2,1:T(8,128)(2,1)} copy(bf16[32,2,16,2048]{0,1,3,2:T(2,128)(2,1)} %bitcast.91) | data formatting | bytes 8388608 | tf_op jit(solution)/shard_map/all_to_all | solution.py:42
  256.5 3.6 fusion.47
  261.3 7.0 %pad_maximum_fusion = bf16[768,2,2048]{2,0,1:T(8,128)(2,1)} fusion(bf16[128,2,2048]{2,0,1:T(8,128)(2,1)S(1)} %bitcast.101, bf16[512,2,2048]{2,0,1:T(8,128)(2,1)S(1)} %bitcast.93, bf16[128,2,2048]{2,0,1:T(8,128)(2,1)S(1)} %bitcast.100), kind=kLoop, calls=%fused_computation.11 | loop fusion | flops 18874368 | bytes 12582912 | tf_op jit(solution)/shard_map/concatenate | solution.py:45
  268.3 23.2 %while.10 = (s32[]{:T(128)}, bf16[4,128,2,2048]{3,1,0,2:T(8,128)(2,1)}, s32[4]{0:T(128)S(1)}, bf16[768,2,2048]{2,0,1:T(8,128)(2,1)}, bf16[2,128,2,384]{3,1,2,0:T...) while((s32[]{:T(128)}, bf16[4,128,2,2048]{3,1,0,2:T(8,128)(2,1)}, s32[4]{0:T(128)S(1)}, ...), condition=%wide.region_1.2_spmd, body=%wide.region_0.1_spmd.sunk | while | flops 805830656 | bytes 8782491 | solution.py:53
  269.5 2.9 fusion.56
  273.0 1.1 constant_dynamic-update-slice_fusion.2
  275.3 2.9 fusion.56
  278.8 1.1 constant_dynamic-update-slice_fusion.2
  281.1 2.9 fusion.56
  284.6 1.1 constant_dynamic-update-slice_fusion.2
  286.9 2.9 fusion.56
  290.4 1.1 constant_dynamic-update-slice_fusion.2
  291.5 6.5 %copy.39 = bf16[512,2,2048]{2,1,0:T(2,128)(2,1)S(1)} copy(bf16[512,2,2048]{2,0,1:T(8,128)(2,1)} %bitcast.102) | data formatting | bytes 8388608 | tf_op jit(solution)/shard_map/reshape | solution.py:54
  298.0 99.6 %all_to_all.33 = bf16[512,2,2048]{2,1,0:T(2,128)(2,1)S(1)} all-to-all(bf16[512,2,2048]{2,1,0:T(2,128)(2,1)S(1)} %copy.39), channel_id=1, replica_groups=mesh['ma'=16,'ch'=2] {'ma'}, dimensions={0} | all-to-all | bytes 8388608 | tf_op jit(solution)/shard_map/all_to_all | solution.py:55
  397.6 5.4 %copy.66 = bf16[16,32,2,2048]{3,0,2,1:T(8,128)(2,1)} copy(bf16[16,32,2,2048]{3,2,1,0:T(2,128)(2,1)S(1)} %bitcast.95) | data formatting | bytes 8388608 | tf_op jit(solution)/shard_map/all_to_all | solution.py:55
  403.0 7.4 %reshape.89 = bf16[32,2,256,128]{3,2,1,0:T(8,128)(2,1)} reshape(bf16[32,2,16,2048]{3,2,1,0:T(8,128)(2,1)} %bitcast.96) | data formatting | bytes 8388608 | tf_op jit(solution)/shard_map/reshape | solution.py:56
  410.4 6.5 %copy.41 = bf16[32,2,256,128]{2,3,1,0:T(8,128)(2,1)} copy(bf16[32,2,256,128]{3,2,1,0:T(8,128)(2,1)} %reshape.89) | data formatting | bytes 8388608 | tf_op jit(solution)/shard_map/reshape | solution.py:56
  416.9 16.5 %all-gather.2.cloned.1.call-done = bf16[32,512,2,128]{1,3,2,0:T(8,128)(2,1)} async-done(((bf16[32,256,2,128]{1,3,2,0:T(8,128)(2,1)}), bf16[32,512,2,128]{1,3,2,0:T(8,128)(2,1)}) %all-gather.2.cloned.1.call-update) | async-done | bytes 8388624 | tf_op jit(solution)/shard_map/all_gather | solution.py:60
  433.4 11.4 %fusion.16 = f32[32,128,2,2,128]{1,4,2,3,0:T(8,128)} fusion(bf16[32,128,2,512,1]{3,2,1,0,4:T(2,128)(2,1)} %bitcast.98, bf16[32,512,2,128]{1,3,2,0:T(8,128)(2,1)} %all-gather.2.cloned.1.call-done), kind=kOutput, calls=%fused_computation.13 | convolution fusion | flops 2147483648 | bytes 25165824 | tf_op jit(solution)/shard_map/mkqc,mcrs->mkqrs/dot_general | solution.py:57
  444.8 2.6 fusion.24
  447.3 2.6 fusion.25
  450.1 3.8 copy.45
  (39 shorter events, 7.7 us)
Async XLA Ops:
  67.8 8.6 %copy-start.2 = (u32[32]{0:T(128)S(1)}, u32[32]{0:T(128)}, u32[]{:S(2)}) copy-start(u32[32]{0:T(128)} %constant.52) | copy-start | bytes 388
  67.8 9.8 %copy-start.1 = (s32[32]{0:T(128)S(1)}, s32[32]{0:T(128)}, u32[]{:S(2)}) copy-start(s32[32]{0:T(128)} %param.7) | copy-start | bytes 388
  67.8 109.6 %all-to-all-start = ((bf16[16,2,65536]{2,1,0:T(2,128)(2,1)}), bf16[16,2,65536]{2,1,0:T(2,128)(2,1)}, u32[]{:S(2)}, u32[]{:S(2)}) async-start(bf16[16,2,65536]{2,1,0:T(2,128)(2,1)} %reshape.107), calls=%async_computation | async-start | bytes 8388608 | tf_op jit(solution)/shard_map/all_to_all | solution.py:42
  76.3 357.1 %all-gather.2.cloned.1.call-start = ((), (), s32[]{:S(2)}) async-start(), calls=%async_computation.2 | async-start | bytes 12582912 | tf_op jit(solution)/shard_map/all_gather | solution.py:60
  256.5 4.7 %copy-start = (bf16[32,2,16,2048]{3,0,2,1:T(8,128)(2,1)S(1)}, bf16[32,2,16,2048]{3,0,2,1:T(8,128)(2,1)}, u32[]{:S(2)}) copy-start(bf16[32,2,16,2048]{3,0,2,1:T(8,128)(2,1)} %copy.51) | copy-start | bytes 12582916
Sparse Core Ops, SparseCore 0:
  417.0 16.2 all-gather.1
where the time goes:
time: 467 us; the launch traced here: 461 us
  blocking collectives  191 us (41%)
  local copies, waits for them, and re-layouts  187 us (40%)
  matrix products  28.3 us (6%)
  waiting for transfers between devices  16.5 us (4%)
  between operations  14.2 us (3%)
  other arithmetic  12.5 us (3%)
  starting transfers between devices  8.56 us (2%)
    all_to_all x1, blocking collectives, on_device(): lax.all_to_all(mixed_columns, 'ma', split_axis=0, concat_axis=2, tiled=True)  99.6 us
    unnamed x1, blocking collectives  91.8 us
    all_to_all x2, local copies, waits for them, and re-layouts, on_device(): lax.all_to_all(flat_rows, 'ma', split_axis=2, concat_axis=0, tiled=True)  63.1 us
    reshape x1, local copies, waits for them, and re-layouts, on_device(): jnp.transpose(visibilities, (0, 2, 1, 3))  40.5 us
    unnamed x13, local copies, waits for them, and re-layouts  38.2 us
    all_gather x1, waiting for transfers between devices, on_device(): lax.all_gather(mixed_rows, 'ch', axis=1, tiled=True)  16.5 us
    reshape x2, local copies, waits for them, and re-layouts, on_device(): returned.reshape(rows_dev, 2, chan_dev, svd_modes)  13.9 us
    dot_general x4, matrix products, convolve(): jnp.einsum('pbqe,eqf->bpf', toeplitz_block, window, preferred_element_typ...  11.7 us
  transfers between devices with their start and end apart: 2, of which 1 were waited for; matrix products, arithmetic and copies ran while one was open for 2% of the time, Pallas kernels for 0%

commit v1 on v0

--- a/solution.py
+++ b/solution.py
@@ -39,7 +39,10 @@
     imag_sum = jnp.dot(sine_table, flag_values, precision=lax.Precision.HIGHEST)
     kernel_taps = (jnp.stack([real_sum, -imag_sum]) / total).astype(jnp.bfloat16)
     flat_rows = jnp.transpose(visibilities, (0, 2, 1, 3)).reshape(rows_dev, 2, chan_dev * svd_modes)
-    columns = lax.all_to_all(flat_rows, "ma", split_axis=2, concat_axis=0, tiled=True)
+    columns = jnp.concatenate(
+        lax.all_to_all(jnp.stack(jnp.split(flat_rows, lax.axis_size("ma"), axis=2)), "ma", 0, 0),
+        axis=0,
+    )
     block_rows = math.gcd(total, 128)
     toeplitz_block = toeplitz(kernel_taps, block_rows)
     wrapped = jnp.concatenate([columns[total - H :], columns, columns[:H]], axis=0)

time: 467 us -> 361 us (0.77); the launches traced: 461 us -> 360 us
  local copies, waits for them, and re-layouts: 187 us -> 85.5 us
    all_to_all x2 -> x1, local copies, waits for them, and re-layouts: 63.1 us -> 2.5 us  [on_device(): lax.all_to_all(jnp.stack(jnp.split(flat_rows, lax.axis_size('ma'), axis=2...]
    reshape x1, local copies, waits for them, and re-layouts: 40.5 us -> 7.31 us  [on_device(): jnp.transpose(visibilities, (0, 2, 1, 3))]
    unnamed x13 -> x24, local copies, waits for them, and re-layouts: 38.2 us -> 26.4 us
    transpose x0 -> x1, local copies, waits for them, and re-layouts: none -> 5.23 us  [on_device(): jnp.transpose(visibilities, (0, 2, 1, 3))]
where the time goes in v1:
time: 361 us; the launch traced here: 360 us
  blocking collectives  191 us (53%)
  local copies, waits for them, and re-layouts  85.5 us (24%)
  matrix products  28.3 us (8%)
  waiting for transfers between devices  16.5 us (5%)
  between operations  14.2 us (4%)
  other arithmetic  12.6 us (3%)
  starting transfers between devices  8.56 us (2%)
    all_to_all x1, blocking collectives, on_device(): lax.all_to_all(mixed_columns, 'ma', split_axis=0, concat_axis=2, tiled=True)  99.6 us
    unnamed x1, blocking collectives  91.7 us
    unnamed x24, local copies, waits for them, and re-layouts  26.4 us
    all_gather x1, waiting for transfers between devices, on_device(): lax.all_gather(mixed_rows, 'ch', axis=1, tiled=True)  16.4 us
    reshape x2, local copies, waits for them, and re-layouts, on_device(): returned.reshape(rows_dev, 2, chan_dev, svd_modes)  13.8 us
    dot_general x4, matrix products, convolve(): jnp.einsum('pbqe,eqf->bpf', toeplitz_block, window, preferred_element_typ...  11.8 us
    dot_general x1, matrix products, on_device(): jnp.einsum('mkqc,mcrs->mkqrs', kl_basis, lax.all_gather(mixed_rows, 'ch',...  11.4 us
    all_to_all x1, starting transfers between devices, on_device(): lax.all_to_all(jnp.stack(jnp.split(flat_rows, lax.axis_size('ma'), axis=2...  8.52 us
  transfers between devices with their start and end apart: 2, of which 1 were waited for; matrix products, arithmetic and copies ran while one was open for 2% of the time, Pallas kernels for 0%

profile of v1, /device:TPU:0, one launch (start us, length us, event | category | flops | bytes accessed | tf_op | source)
XLA Modules:
  0.0 359.7 jit_solution(7885117892029958529)
XLA Ops:
  6.5 5.2 %copy.35 = bf16[32,2,256,128]{3,2,0,1:T(8,128)(2,1)} copy(bf16[32,2,256,128]{3,1,2,0:T(2,128)(2,1)} %bitcast.158) | data formatting | bytes 8388608 | tf_op jit(solution)/shard_map/transpose | solution.py:41
  11.8 7.3 %reshape.90 = bf16[32,2,32768]{2,0,1:T(8,128)(2,1)} reshape(bf16[32,2,256,128]{3,2,0,1:T(8,128)(2,1)} %copy.35) | data formatting | bytes 8388608 | tf_op jit(solution)/shard_map/reshape | solution.py:41
  19.1 1.7 fusion.52
  20.8 1.7 fusion.51
  22.4 1.7 fusion.50
  30.8 1.7 fusion.45
  32.5 1.7 fusion.44
  34.1 1.7 fusion.43
  35.8 1.7 fusion.42
  44.1 1.7 fusion.37
  45.8 8.5 %all-to-all-start = ((bf16[16,32,2,2048]{3,1,2,0:T(8,128)(2,1)}), bf16[16,32,2,2048]{3,1,2,0:T(8,128)(2,1)}, u32[]{:S(2)}, u32[]{:S(2)}) async-start(bf16[16,32,2,2048]{3,1,2,0:T(8,128)(2,1)} %fusion.37), calls=%async_computation | async-start | bytes 8388608 | tf_op jit(solution)/shard_map/all_to_all | solution.py:43
  55.9 91.7 %all-reduce.1 = s32[512]{0:T(512)S(1)} all-reduce(s32[512]{0:T(512)S(1)} %dynamic-update-slice), channel_id=1, replica_groups=mesh['ma'=16,'ch'=2] {'ma'}, use_global_device_ids=true, to_apply=%add.1 | all-reduce | flops 512 | bytes 4096
  147.6 2.6 convolution_reduce_fusion
  150.3 2.5 fusion.30
  155.4 1.7 fusion.63
  157.3 2.5 copy.37
  159.8 7.1 %pad_maximum_fusion = bf16[768,2,2048]{2,0,1:T(8,128)(2,1)} fusion(bf16[128,2,2048]{2,0,1:T(8,128)(2,1)S(1)} %bitcast.157, bf16[512,2,2048]{2,0,1:T(8,128)(2,1)S(1)} %bitcast.151, bf16[128,2,2048]{2,0,1:T(8,128)(2,1)S(1)} %bitcast.156), kind=kLoop, calls=%fused_computation.11 | loop fusion | flops 18874368 | bytes 12582912 | tf_op jit(solution)/shard_map/concatenate | solution.py:48
  166.9 23.6 %while.10 = (s32[]{:T(128)}, bf16[4,128,2,2048]{3,1,0,2:T(8,128)(2,1)}, s32[4]{0:T(128)S(1)}, bf16[768,2,2048]{2,0,1:T(8,128)(2,1)}, bf16[2,128,2,384]{3,1,2,0:T...) while((s32[]{:T(128)}, bf16[4,128,2,2048]{3,1,0,2:T(8,128)(2,1)}, s32[4]{0:T(128)S(1)}, ...), condition=%wide.region_1.2_spmd, body=%wide.region_0.1_spmd.sunk | while | flops 805830656 | bytes 8781991 | solution.py:56
  168.3 2.9 fusion.72
  174.2 2.9 fusion.72
  180.2 2.9 fusion.72
  186.0 2.9 fusion.72
  190.5 6.5 %copy.41 = bf16[512,2,2048]{2,1,0:T(2,128)(2,1)S(1)} copy(bf16[512,2,2048]{2,0,1:T(8,128)(2,1)} %bitcast.159) | data formatting | bytes 8388608 | tf_op jit(solution)/shard_map/reshape | solution.py:57
  197.0 99.6 %all_to_all.20 = bf16[512,2,2048]{2,1,0:T(2,128)(2,1)S(1)} all-to-all(bf16[512,2,2048]{2,1,0:T(2,128)(2,1)S(1)} %copy.41), channel_id=1, replica_groups=mesh['ma'=16,'ch'=2] {'ma'}, dimensions={0} | all-to-all | bytes 8388608 | tf_op jit(solution)/shard_map/all_to_all | solution.py:58
  296.7 5.4 %copy.64 = bf16[16,32,2,2048]{3,0,2,1:T(8,128)(2,1)} copy(bf16[16,32,2,2048]{3,2,1,0:T(2,128)(2,1)S(1)} %bitcast.153) | data formatting | bytes 8388608 | tf_op jit(solution)/shard_map/all_to_all | solution.py:58
  302.1 7.4 %reshape.93 = bf16[32,2,256,128]{3,2,1,0:T(8,128)(2,1)} reshape(bf16[32,2,16,2048]{3,2,1,0:T(8,128)(2,1)} %bitcast.154) | data formatting | bytes 8388608 | tf_op jit(solution)/shard_map/reshape | solution.py:59
  309.5 6.4 %copy.43 = bf16[32,2,256,128]{2,3,1,0:T(8,128)(2,1)} copy(bf16[32,2,256,128]{3,2,1,0:T(8,128)(2,1)} %reshape.93) | data formatting | bytes 8388608 | tf_op jit(solution)/shard_map/reshape | solution.py:59
  315.9 16.4 %all-gather.2.cloned.1.call-done = bf16[32,512,2,128]{1,3,2,0:T(8,128)(2,1)} async-done(((bf16[32,256,2,128]{1,3,2,0:T(8,128)(2,1)}), bf16[32,512,2,128]{1,3,2,0:T(8,128)(2,1)}) %all-gather.2.cloned.1.call-update) | async-done | bytes 8388624 | tf_op jit(solution)/shard_map/all_gather | solution.py:63
  332.4 11.4 %fusion.16 = f32[32,128,2,2,128]{1,4,2,3,0:T(8,128)} fusion(bf16[32,128,2,512,1]{3,2,1,0,4:T(2,128)(2,1)} %bitcast.155, bf16[32,512,2,128]{1,3,2,0:T(8,128)(2,1)} %all-gather.2.cloned.1.call-done), kind=kOutput, calls=%fused_computation.13 | convolution fusion | flops 2147483648 | bytes 25165824 | tf_op jit(solution)/shard_map/mkqc,mcrs->mkqrs/dot_general | solution.py:60
  343.7 2.6 fusion.25
  346.3 2.6 fusion.24
  349.1 3.8 %copy.47 = bf16[32,128,2,128]{3,2,1,0:T(2,128)(2,1)} copy(bf16[32,128,2,128]{1,3,0,2:T(8,128)(2,1)S(1)} %pad_maximum_fusion.1) | data formatting | bytes 4194304 | tf_op jit(solution)/shard_map/stack | solution.py:68
  (51 shorter events, 26.3 us)
Async XLA Ops:
  45.8 8.6 %copy-start.1 = (u32[32]{0:T(128)S(1)}, u32[32]{0:T(128)}, u32[]{:S(2)}) copy-start(u32[32]{0:T(128)} %constant.52) | copy-start | bytes 388
  45.8 9.8 %copy-start = (s32[32]{0:T(128)S(1)}, s32[32]{0:T(128)}, u32[]{:S(2)}) copy-start(s32[32]{0:T(128)} %param.7) | copy-start | bytes 388
  45.8 109.6 %all-to-all-start = ((bf16[16,32,2,2048]{3,1,2,0:T(8,128)(2,1)}), bf16[16,32,2,2048]{3,1,2,0:T(8,128)(2,1)}, u32[]{:S(2)}, u32[]{:S(2)}) async-start(bf16[16,32,2,2048]{3,1,2,0:T(8,128)(2,1)} %fusion.37), calls=%async_computation | async-start | bytes 8388608 | tf_op jit(solution)/shard_map/all_to_all | solution.py:43
  54.4 278.0 %all-gather.2.cloned.1.call-start = ((), (), s32[]{:S(2)}) async-start(), calls=%async_computation.2 | async-start | bytes 12582912 | tf_op jit(solution)/shard_map/all_gather | solution.py:63
Sparse Core Ops, SparseCore 0:
  316.0 16.2 all-gather.1
